TPU v7x, 128 devices: a whole 4x4x4 slice. The times are simulated.
128 devices in a mesh: req: 8 (over z, core), seq: 16 (over x, y).
Axes of the slice: x: 4, y: 4, z: 4, core: 2. Of those that a mesh axis runs over, the one named last changes fastest.
Arguments:
- token_ids: int32 [64, 4], replicated, may hold values from 0 to 127999, as said below
- embed_table: bfloat16 [128000, 1024], P(('req', 'seq')), may hold values from -6 to 6
- ln_gains: float32 [4, 1024], replicated, may hold values from 0.25 to 1.75
- ln_biases: float32 [4, 1024], replicated, may hold values from -1.5 to 1.5
- rel_table: bfloat16 [512, 1024], replicated, may hold values from -6 to 6
- w_qkv: bfloat16 [1024, 3072], replicated, may hold values from -0.1875 to 0.1875
- w_out: bfloat16 [1024, 1024], replicated, may hold values from -0.1875 to 0.1875
- cache_keys: bfloat16 [64, 8192, 1024], P('req', 'seq'), may hold values from -3000 to 3000
- cache_values: bfloat16 [64, 8192, 1024], P('req', 'seq'), may hold values from -6 to 6
- lengths: int32 [64], P('req'), may hold values from 129 to 8192, as said below
- window_starts: int32 [64], P('req'), may hold values from 4 to 4096, as said below
- cache_buckets: int32 [64, 4, 8192], P('req', None, 'seq'), may hold values from 0 to 511
- new_buckets: int32 [64, 4, 4], P('req'), may hold values from 0 to 511
- w_in: bfloat16 [4096, 1024], P('seq'), may hold values from -0.1875 to 0.1875
- w_down: bfloat16 [4096, 1024], P('seq'), may hold values from -0.09375 to 0.09375
Outputs:
- layer_out: bfloat16 [64, 4, 1024], P('req')
Inputs may be any that keep to these rules, and one draw needn't show every extreme that they name: `token_ids`: every aligned block of 1000 ids holds the id of at least one new token. `lengths`: some request has length 8192. window_starts = max(4, lengths - 4096) for each request.
All inputs are finite; a program needn't handle non-finite values.
Results may differ from a plain program's by a relative error of at most 0.018.
Values may be sent and summed in bfloat16 or wider, within the bound.
A program may use at most 192 MiB of HBM per device.

v0:
```python
import math
import jax
import jax.numpy as jnp
from jax import lax
from jax.sharding import PartitionSpec as P

HEADS = 16
HEAD_DIM = 64
SINKS = 4
norm_epsilon = 1e-06
masked_score = -1e30


def layer_norm(values, gain, shift):
    center = values - jnp.mean(values, axis=-1, keepdims=True)
    spread = jnp.mean(center * center, axis=-1, keepdims=True)
    return center * lax.rsqrt(spread + norm_epsilon) * gain + shift


def expand_rows(rows_x, in_rows, down_rows):
    inner = lax.dot_general(
        rows_x, in_rows, (((1,), (1,)), ((), ())), preferred_element_type=jnp.float32
    )
    inner = jax.nn.gelu(inner, approximate=False).astype(jnp.bfloat16)
    return jnp.dot(inner, down_rows, preferred_element_type=jnp.float32)


def shards(
    token_ids,
    embed_table,
    ln_gains,
    ln_biases,
    rel_table,
    w_qkv,
    w_out,
    cache_keys,
    cache_values,
    lengths,
    window_starts,
    cache_buckets,
    new_buckets,
    w_in,
    w_down,
):
    group_reqs, piece_len, width = cache_keys.shape
    new_count = token_ids.shape[1]
    vocab_rows = embed_table.shape[0]
    bucket_count = rel_table.shape[0]
    group_rows = group_reqs * new_count
    seq_index = lax.axis_index("seq")
    req_index = lax.axis_index("req")
    owner_index = req_index * lax.axis_size("seq") + seq_index
    local_ids = token_ids.reshape(-1) - owner_index * vocab_rows
    one_hot = (local_ids[:, None] == jnp.arange(vocab_rows, dtype=jnp.int32)[None, :]).astype(
        jnp.bfloat16
    )
    looked_up = jnp.dot(one_hot, embed_table, preferred_element_type=jnp.float32)
    summed = lax.psum(looked_up, ("req", "seq"))
    own_rows = lax.dynamic_slice_in_dim(summed, req_index * group_rows, group_rows, 0)
    hidden_zero = layer_norm(own_rows, ln_gains[0], ln_biases[0]).astype(jnp.bfloat16)
    relative = layer_norm(rel_table.astype(jnp.float32), ln_gains[3], ln_biases[3]).astype(
        jnp.bfloat16
    )
    pos_query = jnp.dot(relative, w_qkv[:, :width], preferred_element_type=jnp.float32).astype(
        jnp.bfloat16
    )
    pos_key = jnp.dot(
        relative, w_qkv[:, width : 2 * width], preferred_element_type=jnp.float32
    ).astype(jnp.bfloat16)
    projected = jnp.dot(hidden_zero, w_qkv, preferred_element_type=jnp.float32).astype(jnp.bfloat16)
    queries = projected[:, :width].reshape(group_reqs, new_count, HEADS, HEAD_DIM)
    fresh_keys = projected[:, width : 2 * width].reshape(group_reqs, new_count, HEADS, HEAD_DIM)
    fresh_values = projected[:, 2 * width :].reshape(group_reqs, new_count, HEADS, HEAD_DIM)
    pos_key_heads = pos_key.reshape(bucket_count, HEADS, HEAD_DIM)
    reversed_query_heads = pos_query[::-1].reshape(bucket_count, HEADS, HEAD_DIM)
    query_table = jnp.einsum(
        "rthd,bhd->rhtb", queries, pos_key_heads, preferred_element_type=jnp.float32
    )
    score_scale = 1.0 / math.sqrt(3 * HEAD_DIM)
    bucket_range = jnp.arange(bucket_count, dtype=jnp.int32)
    first_place = seq_index * piece_len
    positions = first_place + jnp.arange(piece_len, dtype=jnp.int32)
    piece_live = (first_place < lengths) & (
        (first_place < SINKS) | (first_place + piece_len > window_starts)
    )
    key_heads = cache_keys.reshape(group_reqs, piece_len, HEADS, HEAD_DIM)
    value_heads = cache_values.reshape(group_reqs, piece_len, HEADS, HEAD_DIM)

    def piece_scores(queries_one, table_one, keys_one, buckets_one, length_one, start_one):
        content = jnp.einsum(
            "thd,phd->htp", queries_one, keys_one, preferred_element_type=jnp.float32
        )
        selector = (buckets_one[:, :, None] == bucket_range[None, None, :]).astype(jnp.float32)
        to_pos = jnp.einsum("tpb,htb->htp", selector, table_one, precision=lax.Precision.HIGHEST)
        key_table = jnp.einsum(
            "phd,bhd->hpb", keys_one, reversed_query_heads, preferred_element_type=jnp.float32
        )
        from_pos = jnp.einsum("tpb,hpb->htp", selector, key_table, precision=lax.Precision.HIGHEST)
        allowed = (positions < length_one) & ((positions < SINKS) | (positions >= start_one))
        return jnp.where(
            allowed[None, None, :], (content + to_pos + from_pos) * score_scale, masked_score
        )

    def score_step(items):
        queries_one, table_one, keys_one, buckets_one, length_one, start_one, live_one = items
        return piece_scores(queries_one, table_one, keys_one, buckets_one, length_one, start_one)

    scores = lax.map(
        score_step,
        (queries, query_table, key_heads, cache_buckets, lengths, window_starts, piece_live),
    )
    content_new = jnp.einsum(
        "rthd,ruhd->rhtu", queries, fresh_keys, preferred_element_type=jnp.float32
    )
    to_pos_new = jnp.take_along_axis(
        query_table,
        jnp.broadcast_to(new_buckets[:, None], (group_reqs, HEADS, new_count, new_count)),
        axis=3,
    )
    gathered_new = jnp.take(pos_query, bucket_count - 1 - new_buckets, axis=0).reshape(
        group_reqs, new_count, new_count, HEADS, HEAD_DIM
    )
    from_pos_new = jnp.einsum(
        "rtuhd,ruhd->rhtu", gathered_new, fresh_keys, preferred_element_type=jnp.float32
    )
    causal = jnp.arange(new_count)[None, :] <= jnp.arange(new_count)[:, None]
    fresh_scores = jnp.where(
        causal, (content_new + to_pos_new + from_pos_new) * score_scale, masked_score
    )
    row_max = jnp.maximum(lax.pmax(jnp.max(scores, axis=-1), "seq"), jnp.max(fresh_scores, axis=-1))

    def weigh_piece(scores_one, max_one, values_one):
        exp_terms = jnp.exp(scores_one - max_one[:, :, None])
        numerator = jnp.einsum(
            "htp,phd->thd",
            exp_terms.astype(jnp.bfloat16),
            values_one,
            preferred_element_type=jnp.float32,
        )
        return (numerator, jnp.sum(exp_terms, axis=-1))

    def weigh_step(items):
        scores_one, max_one, values_one, live_one = items
        return weigh_piece(scores_one, max_one, values_one)

    numerators, denominators = lax.map(weigh_step, (scores, row_max, value_heads, piece_live))
    numer_total, denom_total = lax.psum((numerators, denominators), "seq")
    fresh_exp = jnp.exp(fresh_scores - row_max[..., None])
    fresh_numer = jnp.einsum(
        "rhtu,ruhd->rthd",
        fresh_exp.astype(jnp.bfloat16),
        fresh_values,
        preferred_element_type=jnp.float32,
    )
    denom_all = jnp.transpose(denom_total + jnp.sum(fresh_exp, axis=-1), (0, 2, 1))
    attended = (
        ((numer_total + fresh_numer) / denom_all[..., None])
        .astype(jnp.bfloat16)
        .reshape(group_rows, width)
    )
    attn_out = jnp.dot(attended, w_out, preferred_element_type=jnp.float32)
    hidden_one = layer_norm(
        hidden_zero.astype(jnp.float32) + attn_out, ln_gains[1], ln_biases[1]
    ).astype(jnp.bfloat16)
    partial_mlp = expand_rows(hidden_one, w_in, w_down)
    mlp_out = lax.psum(partial_mlp.astype(jnp.bfloat16), "seq").astype(jnp.float32)
    layer_out = layer_norm(
        hidden_one.astype(jnp.float32) + mlp_out, ln_gains[2], ln_biases[2]
    ).astype(jnp.bfloat16)
    return layer_out.reshape(group_reqs, new_count, width)


def solution(mesh):
    in_specs = (
        P(),
        P(("req", "seq"), None),
        P(),
        P(),
        P(),
        P(),
        P(),
        P("req", "seq", None),
        P("req", "seq", None),
        P("req"),
        P("req"),
        P("req", None, "seq"),
        P("req", None, None),
        P("seq", None),
        P("seq", None),
    )
    out_specs = P("req", None, None)
    return jax.shard_map(shards, mesh=mesh, in_specs=in_specs, out_specs=out_specs, check_vma=False)
```

profile of v0, /device:TPU:0, one launch (start us, length us, event | category | flops | bytes accessed | tf_op | source)
XLA Modules:
  0.0 749.9 jit_solution(12523177118049195866)
XLA Ops:
  7.6 3.4 fusion.55
  13.0 2.9 fusion.49
  16.0 3.9 fusion.46
  20.9 10.3 %rev.3 = bf16[512,1024]{1,0:T(8,128)(2,1)} reverse(bf16[512,1024]{1,0:T(8,128)(2,1)S(1)} %fusion.49), dimensions={0} | reverse | bytes 2097152 | tf_op jit(solution)/shard_map/rev | solution.py:75
  32.1 2.3 copy.113
  34.7 2.3 copy.111
  37.0 11.4 %copy.110 = bf16[8,512,1024]{1,2,0:T(8,128)(2,1)} copy(bf16[8,512,1024]{2,1,0:T(8,128)(2,1)} %param.26) | data formatting | bytes 16777216 | tf_op args[7]
  48.5 11.4 %copy.109 = bf16[8,512,1024]{1,2,0:T(8,128)(2,1)} copy(bf16[8,512,1024]{2,1,0:T(8,128)(2,1)} %param.27) | data formatting | bytes 16777216 | tf_op args[8]
  60.6 100.8 %all-reduce.4.cloned.1.call-done = f32[256,1024]{1,0:T(8,128)} async-done(((f32[256,1024]{1,0:T(8,128)}), f32[256,1024]{1,0:T(8,128)}) %all-reduce.4.cloned.1.call-update) | async-done | bytes 1048592 | tf_op jit(solution)/shard_map/psum | solution.py:58
  163.6 4.1 convolution_convert_fusion
  172.7 19.5 %gather_fusion.1 = f32[2048]{0:T(1024)S(1)} fusion(f32[8,16,4,512]{3,0,2,1:T(8,128)S(1)} %convolution_bitcast_fusion.1, s32[2048]{0:T(1024)S(1)} %reshape.131), kind=kCustom, calls=%fused_computation.1 | custom fusion | bytes 49152 | tf_op jit(solution)/shard_map/jit(take_along_axis)/gather | solution.py:115
  195.7 272.9 %while.24 = (s32[]{:T(128)}, f32[8,16,4,512]{3,2,1,0:T(4,128)}, s32[8]{0:T(128)}, s32[8]{0:T(128)}, bf16[8,4,16,64]{3,1,2,0:T(4,128)(2,1)}, /*index=5*/bf16[8,51...) while((s32[]{:T(128)}, f32[8,16,4,512]{3,2,1,0:T(4,128)}, ...), condition=%wide.region_6.7_spmd.clone, body=%wide.region_5.6_spmd.clone.sunk | while | flops 945949696 | bytes 44370624 | solution.py:108
  201.1 1.6 iota_compare_fusion.8
  202.8 2.6 fusion.190
  205.4 3.6 fusion.188
  209.0 17.1 %fusion.189 = f32[512,16,4]{1,2,0:T(4,128)} fusion(f32[16,512,512]{2,1,0:T(8,128)S(1)} %fusion.188, s32[4,512]{0,1:T(8,128)S(1)} %bitcast.130), kind=kOutput, calls=%fused_computation.16.clone.1 | convolution fusion | flops 202375168 | bytes 16916480 | tf_op jit(solution)/shard_map/while/body/eval_jaxpr/tpb,hpb->htp/dot_general | solution.py:98
  227.7 2.1 fusion.192
  235.3 1.6 iota_compare_fusion.8
  236.9 2.6 fusion.190
  239.5 3.6 fusion.188
  243.1 17.1 %fusion.189 = f32[512,16,4]{1,2,0:T(4,128)} fusion(f32[16,512,512]{2,1,0:T(8,128)S(1)} %fusion.188, s32[4,512]{0,1:T(8,128)S(1)} %bitcast.130), kind=kOutput, calls=%fused_computation.16.clone.1 | convolution fusion | flops 202375168 | bytes 16916480 | tf_op jit(solution)/shard_map/while/body/eval_jaxpr/tpb,hpb->htp/dot_general | solution.py:98
  261.8 2.2 fusion.192
  269.4 1.6 iota_compare_fusion.8
  271.0 2.6 fusion.190
  273.6 3.6 fusion.188
  277.3 17.1 %fusion.189 = f32[512,16,4]{1,2,0:T(4,128)} fusion(f32[16,512,512]{2,1,0:T(8,128)S(1)} %fusion.188, s32[4,512]{0,1:T(8,128)S(1)} %bitcast.130), kind=kOutput, calls=%fused_computation.16.clone.1 | convolution fusion | flops 202375168 | bytes 16916480 | tf_op jit(solution)/shard_map/while/body/eval_jaxpr/tpb,hpb->htp/dot_general | solution.py:98
  295.9 2.1 fusion.192
  303.5 1.6 iota_compare_fusion.8
  305.1 2.6 fusion.190
  307.8 3.6 fusion.188
  311.4 17.1 %fusion.189 = f32[512,16,4]{1,2,0:T(4,128)} fusion(f32[16,512,512]{2,1,0:T(8,128)S(1)} %fusion.188, s32[4,512]{0,1:T(8,128)S(1)} %bitcast.130), kind=kOutput, calls=%fused_computation.16.clone.1 | convolution fusion | flops 202375168 | bytes 16916480 | tf_op jit(solution)/shard_map/while/body/eval_jaxpr/tpb,hpb->htp/dot_general | solution.py:98
  330.0 2.2 fusion.192
  337.6 1.6 iota_compare_fusion.8
  339.2 2.6 fusion.190
  341.9 3.6 fusion.188
  345.5 17.1 %fusion.189 = f32[512,16,4]{1,2,0:T(4,128)} fusion(f32[16,512,512]{2,1,0:T(8,128)S(1)} %fusion.188, s32[4,512]{0,1:T(8,128)S(1)} %bitcast.130), kind=kOutput, calls=%fused_computation.16.clone.1 | convolution fusion | flops 202375168 | bytes 16916480 | tf_op jit(solution)/shard_map/while/body/eval_jaxpr/tpb,hpb->htp/dot_general | solution.py:98
  364.2 2.1 fusion.192
  371.7 1.6 iota_compare_fusion.8
  373.4 2.6 fusion.190
  376.0 3.6 fusion.188
  379.6 17.1 %fusion.189 = f32[512,16,4]{1,2,0:T(4,128)} fusion(f32[16,512,512]{2,1,0:T(8,128)S(1)} %fusion.188, s32[4,512]{0,1:T(8,128)S(1)} %bitcast.130), kind=kOutput, calls=%fused_computation.16.clone.1 | convolution fusion | flops 202375168 | bytes 16916480 | tf_op jit(solution)/shard_map/while/body/eval_jaxpr/tpb,hpb->htp/dot_general | solution.py:98
  398.3 2.2 fusion.192
  407.5 2.6 fusion.190
  410.1 3.6 fusion.188
  413.7 17.1 %fusion.189 = f32[512,16,4]{1,2,0:T(4,128)} fusion(f32[16,512,512]{2,1,0:T(8,128)S(1)} %fusion.188, s32[4,512]{0,1:T(8,128)S(1)} %bitcast.130), kind=kOutput, calls=%fused_computation.16.clone.1 | convolution fusion | flops 202375168 | bytes 16916480 | tf_op jit(solution)/shard_map/while/body/eval_jaxpr/tpb,hpb->htp/dot_general | solution.py:98
  432.4 2.2 fusion.192
  441.6 2.6 fusion.190
  444.2 3.6 fusion.188
  447.8 17.1 %fusion.189 = f32[512,16,4]{1,2,0:T(4,128)} fusion(f32[16,512,512]{2,1,0:T(8,128)S(1)} %fusion.188, s32[4,512]{0,1:T(8,128)S(1)} %bitcast.130), kind=kOutput, calls=%fused_computation.16.clone.1 | convolution fusion | flops 202375168 | bytes 16916480 | tf_op jit(solution)/shard_map/while/body/eval_jaxpr/tpb,hpb->htp/dot_general | solution.py:98
  466.5 2.2 fusion.192
  470.1 73.2 %pmax.7 = f32[8,16,4]{2,1,0:T(8,128)S(1)} all-reduce(f32[8,16,4]{2,1,0:T(8,128)S(1)} %reduce_max.18), channel_id=1, replica_groups=mesh['req'=8,'seq'=16] {'seq'}, use_global_device_ids=true, to_apply=%region_8.9 | all-reduce | flops 512 | bytes 4096 | tf_op jit(solution)/shard_map/pmax | solution.py:130
  546.8 28.4 %while.23 = (s32[]{:T(128)}, f32[8,4,16,64]{3,1,2,0:T(4,128)}, f32[8,16,4]{1,2,0:T(4,128)S(1)}, bf16[8,512,16,64]{1,3,2,0:T(8,128)(2,1)}, f32[8,16,4,512]{3,2,1,0:T(4,128)}, /*index=5*/f32[8,16,4]{1,2,0:T(4,128)S(1)}, s32[]{:T(128)}) while((s32[]{:T(128)}, f32[8,4,16,64]{3,1,2,0:T(4,128)}, f32[8,16,4]{1,2,0:T(4,128)S(1)}, ...), condition=%wide.region_12.13_spmd, body=%wide.region_10.12_spmd.sunk | while | flops 4325314 | bytes 1351521 | solution.py:146
  548.1 2.3 fusion.180
  551.6 2.3 fusion.180
  555.2 2.3 fusion.180
  558.7 2.3 fusion.180
  562.3 2.3 fusion.180
  565.8 2.3 fusion.180
  569.4 2.3 fusion.180
  572.9 2.3 fusion.180
  575.4 69.6 %psum.30 = f32[8,16,4]{2,1,0:T(8,128)S(1)} all-reduce(f32[8,16,4]{2,1,0:T(8,128)S(1)} %copy.129), channel_id=1, replica_groups=mesh['req'=8,'seq'=16] {'seq'}, use_global_device_ids=true, to_apply=%region_14.15 | all-reduce | flops 512 | bytes 4096 | tf_op jit(solution)/shard_map/psum | solution.py:147
  645.0 8.7 %all-reduce.6.cloned.1.call-done = f32[8,4,16,64]{3,1,2,0:T(4,128)} async-done(((f32[8,4,16,64]{3,1,2,0:T(4,128)}), f32[8,4,16,64]{3,1,2,0:T(4,128)}) %all-reduce.6.cloned.1.call-update) | async-done | bytes 131088 | tf_op jit(solution)/shard_map/psum | solution.py:147
  657.0 2.3 convolution_convert_fusion.1
  659.3 80.3 %all-reduce.8.cloned.1.call-done = bf16[32,1024]{1,0:T(8,128)(2,1)} async-done(((bf16[32,1024]{1,0:T(8,128)(2,1)}), bf16[32,1024]{1,0:T(8,128)(2,1)}) %all-reduce.8.cloned.1.call-update) | async-done | bytes 65552 | tf_op jit(solution)/shard_map/psum | solution.py:166
  (230 shorter events, 97.2 us)
Async XLA Ops:
  6.5 648.7 %copy-start = (bf16[1024,1024]{1,0:T(8,128)(2,1)S(1)}, bf16[1024,1024]{1,0:T(8,128)(2,1)}, u32[]{:S(2)}) copy-start(bf16[1024,1024]{1,0:T(8,128)(2,1)} %param.25) | copy-start | bytes 6291460
  6.5 154.9 %all-reduce.4.cloned.1.call-start = ((), (), s32[]{:S(2)}) async-start(), calls=%async_computation | async-start | bytes 2097152 | tf_op jit(solution)/shard_map/psum | solution.py:58
  7.6 3.5 copy-start.4
  7.6 3.6 copy-start.2
  11.0 0.8 copy-start.16
  11.0 1.4 copy-start.17
  11.0 642.7 %all-reduce.6.cloned.1.call-start = ((), (), s32[]{:S(2)}) async-start(), calls=%async_computation.1 | async-start | bytes 524288 | tf_op jit(solution)/shard_map/psum | solution.py:147
  11.1 2.0 copy-start.3
  11.1 8.8 %copy-start.12 = (pred[8,4,4]{0,2,1:T(4,128)(4,1)}, pred[8,4,4]{0,2,1:T(4,128)(4,1)S(1)}, u32[]{:S(2)}) copy-start(pred[8,4,4]{0,2,1:T(4,128)(4,1)S(1)} %get-tuple-element.221) | copy-start | bytes 388
  11.2 8.7 %copy-start.5 = (s32[8,4,4]{0,2,1:T(4,128)}, s32[8,4,4]{0,2,1:T(4,128)S(1)}, u32[]{:S(2)}) copy-start(s32[8,4,4]{0,2,1:T(4,128)S(1)} %get-tuple-element.223) | copy-start | bytes 1540
  12.4 151.1 %copy-start.8 = (f32[1,1024]{1,0:T(1,128)}, f32[1,1024]{1,0:T(1,128)S(1)}, u32[]{:S(2)}) copy-start(f32[1,1024]{1,0:T(1,128)S(1)} %get-tuple-element.215) | copy-start | bytes 12292
  13.0 150.5 %copy-start.10 = (f32[1,1024]{1,0:T(1,128)}, f32[1,1024]{1,0:T(1,128)S(1)}, u32[]{:S(2)}) copy-start(f32[1,1024]{1,0:T(1,128)S(1)} %get-tuple-element.219) | copy-start | bytes 12292
  162.4 5.3 copy-start.18
  163.6 4.2 copy-start.20
  201.1 4.3 copy-start.1
  235.2 4.3 copy-start.1
  269.4 4.3 copy-start.1
  303.5 4.3 copy-start.1
  337.6 4.3 copy-start.1
  371.7 4.3 copy-start.1
  405.8 4.3 copy-start.1
  440.0 4.3 copy-start.1
  468.7 78.1 %copy-start.15 = (f32[8,16,4]{1,2,0:T(4,128)S(1)}, f32[8,16,4]{1,2,0:T(4,128)}, u32[]{:S(2)}) copy-start(f32[8,16,4]{1,2,0:T(4,128)} %custom-call.5) | copy-start | bytes 6148
  575.2 80.0 %copy-start.9 = (f32[1,1024]{1,0:T(1,128)S(1)}, f32[1,1024]{1,0:T(1,128)}, u32[]{:S(2)}) copy-start(f32[1,1024]{1,0:T(1,128)} %copy-done.8) | copy-start | bytes 12292
  575.2 80.0 %copy-start.11 = (f32[1,1024]{1,0:T(1,128)S(1)}, f32[1,1024]{1,0:T(1,128)}, u32[]{:S(2)}) copy-start(f32[1,1024]{1,0:T(1,128)} %copy-done.10) | copy-start | bytes 12292
  575.2 80.0 %copy-start.19 = (f32[32]{0:T(128)S(1)}, f32[32]{0:T(128)}, u32[]{:S(2)}) copy-start(f32[32]{0:T(128)} %copy-done.18) | copy-start | bytes 388
  575.2 80.0 %copy-start.21 = (f32[32]{0:T(128)S(1)}, f32[32]{0:T(128)}, u32[]{:S(2)}) copy-start(f32[32]{0:T(128)} %copy-done.20) | copy-start | bytes 388
  575.2 164.4 %all-reduce.8.cloned.1.call-start = ((), (), s32[]{:S(2)}) async-start(), calls=%async_computation.2 | async-start | bytes 131072 | tf_op jit(solution)/shard_map/psum | solution.py:166
  655.0 2.0 copy-start.6
  655.0 2.0 copy-start.7
  655.0 2.0 copy-start.22
  655.2 86.5 %copy-start.13 = (f32[1,1024]{1,0:T(1,128)S(1)}, f32[1,1024]{1,0:T(1,128)}, u32[]{:S(2)}) copy-start(f32[1,1024]{1,0:T(1,128)} %get-tuple-element.213) | copy-start | bytes 12292
  655.3 86.5 %copy-start.14 = (f32[1,1024]{1,0:T(1,128)S(1)}, f32[1,1024]{1,0:T(1,128)}, u32[]{:S(2)}) copy-start(f32[1,1024]{1,0:T(1,128)} %get-tuple-element.217) | copy-start | bytes 12292
Sparse Core Ops, SparseCore 0:
  12.2 149.2 all-reduce.3
  575.4 78.3 all-reduce.5
  659.4 80.1 all-reduce.7
where the time goes:
time: 753 us; the launch traced here: 750 us
  matrix products  244 us (32%)
  waiting for transfers between devices  190 us (25%)
  blocking collectives  143 us (19%)
  local copies, waits for them, and re-layouts  115 us (15%)
  other arithmetic  44.1 us (6%)
  between operations  13.6 us (2%)
    dot_general x8, matrix products, piece_scores(): jnp.einsum('tpb,hpb->htp', selector, key_table, precision=lax.Precision.H...  137 us
    psum x1, waiting for transfers between devices, shards(): summed = lax.psum(looked_up, ('req', 'seq'))  101 us
    psum x1, waiting for transfers between devices, shards(): lax.psum(partial_mlp.astype(jnp.bfloat16), 'seq').astype(jnp.float32)  80.3 us
    pmax x1, blocking collectives, shards(): lax.pmax(jnp.max(scores, axis=-1), 'seq')  73.2 us
    psum x1, blocking collectives, shards(): numer_total, denom_total = lax.psum((numerators, denominators), 'seq')  69.6 us
    dynamic_slice x40, local copies, waits for them, and re-layouts, shards(): lax.map(score_step, (queries, query_table, key_heads, cache_buckets, leng...  33.2 us
    dot_general x8, matrix products, piece_scores(): jnp.einsum('phd,bhd->hpb', keys_one, reversed_query_heads, preferred_elem...  28.9 us
    unnamed x49, local copies, waits for them, and re-layouts  24.5 us
  transfers between devices with their start and end apart: 3, of which 3 were waited for; matrix products, arithmetic and copies ran while one was open for 7% of the time, Pallas kernels for 0%

commit v1 on v0

--- a/solution.py
+++ b/solution.py
@@ -55,7 +55,7 @@
         jnp.bfloat16
     )
     looked_up = jnp.dot(one_hot, embed_table, preferred_element_type=jnp.float32)
-    summed = lax.psum(looked_up, ("req", "seq"))
+    summed = lax.all_gather(looked_up, ("req", "seq")).sum(axis=0)
     own_rows = lax.dynamic_slice_in_dim(summed, req_index * group_rows, group_rows, 0)
     hidden_zero = layer_norm(own_rows, ln_gains[0], ln_biases[0]).astype(jnp.bfloat16)
     relative = layer_norm(rel_table.astype(jnp.float32), ln_gains[3], ln_biases[3]).astype(

time: 753 us -> 1080 us (1.43)
  waiting for transfers between devices: 190 us -> 393 us
  matrix products: 244 us -> 346 us
  other arithmetic: 44.1 us -> 83.9 us
  local copies, waits for them, and re-layouts: 115 us -> 100 us
    all_gather x0 -> x1, waiting for transfers between devices: none -> 235 us  [shards(): summed = lax.all_gather(looked_up, ('req', 'seq')).sum(axis=0)]
    psum x1 -> x0, waiting for transfers between devices: 101 us -> none  [shards(): summed = lax.psum(looked_up, ('req', 'seq'))]
    psum x1, waiting for transfers between devices: 8.71 us -> 77.9 us  [shards(): numer_total, denom_total = lax.psum((numerators, denominators), 'seq')]
    dot_general x8, matrix products: 137 us -> 197 us  [piece_scores(): jnp.einsum('tpb,hpb->htp', selector, key_table, precision=lax.Precision.H...]
    dot_general x8, matrix products: 28.9 us -> 77.1 us  [piece_scores(): jnp.einsum('phd,bhd->hpb', keys_one, reversed_query_heads, preferred_elem...]
    reduce_sum x0 -> x1, other arithmetic: none -> 40.6 us  [shards(): summed = lax.all_gather(looked_up, ('req', 'seq')).sum(axis=0)]
    dynamic_slice x40, local copies, waits for them, and re-layouts: 33.2 us -> 17.6 us  [shards(): lax.map(score_step, (queries, query_table, key_heads, cache_buckets, leng...]
    unnamed x49 -> x51, local copies, waits for them, and re-layouts: 24.5 us -> 25.8 us
  transfers between devices with their start and end apart: 3 -> 3, of which waited for: 3 -> 3; matrix products, arithmetic and copies ran while one was open for 7% -> 5% of each run, Pallas kernels for 0% -> 0%
where the time goes in v1:
time: 1080 us
  waiting for transfers between devices  393 us (36%)
  matrix products  346 us (32%)
  blocking collectives  144 us (13%)
  local copies, waits for them, and re-layouts  100 us (9%)
  other arithmetic  83.9 us (8%)
  between operations  13.5 us (1%)
    all_gather x1, waiting for transfers between devices, shards(): summed = lax.all_gather(looked_up, ('req', 'seq')).sum(axis=0)  235 us
    dot_general x8, matrix products, piece_scores(): jnp.einsum('tpb,hpb->htp', selector, key_table, precision=lax.Precision.H...  197 us
    psum x1, waiting for transfers between devices, shards(): lax.psum(partial_mlp.astype(jnp.bfloat16), 'seq').astype(jnp.float32)  80.3 us
    psum x1, waiting for transfers between devices, shards(): numer_total, denom_total = lax.psum((numerators, denominators), 'seq')  77.9 us
    dot_general x8, matrix products, piece_scores(): jnp.einsum('phd,bhd->hpb', keys_one, reversed_query_heads, preferred_elem...  77.1 us
    pmax x1, blocking collectives, shards(): lax.pmax(jnp.max(scores, axis=-1), 'seq')  74.3 us
    psum x1, blocking collectives, shards(): numer_total, denom_total = lax.psum((numerators, denominators), 'seq')  69.6 us
    reduce_sum x1, other arithmetic, shards(): summed = lax.all_gather(looked_up, ('req', 'seq')).sum(axis=0)  40.6 us
  transfers between devices with their start and end apart: 3, of which 3 were waited for; matrix products, arithmetic and copies ran while one was open for 5% of the time, Pallas kernels for 0%

profile of v1, /device:TPU:0, one launch (start us, length us, event | category | flops | bytes accessed | tf_op | source)
XLA Modules:
  0.0 1081.1 jit_solution(12963132022805794936)
XLA Ops:
  7.6 3.4 fusion.55
  13.0 3.9 fusion.46
  16.9 2.3 copy.111
  20.7 3.2 fusion.49
  23.9 10.3 rev.3
  35.5 2.3 copy.113
  37.8 11.4 %copy.110 = bf16[8,512,1024]{1,2,0:T(8,128)(2,1)} copy(bf16[8,512,1024]{2,1,0:T(8,128)(2,1)} %param.26) | data formatting | bytes 16777216 | tf_op args[7]
  49.3 11.6 %copy.109 = bf16[8,512,1024]{1,2,0:T(8,128)(2,1)} copy(bf16[8,512,1024]{2,1,0:T(8,128)(2,1)} %param.27) | data formatting | bytes 16777216 | tf_op args[8]
  62.4 234.6 %all-gather.3.cloned.1.call-done = f32[32768,1024]{1,0:T(8,128)} async-done(((f32[256,1024]{1,0:T(8,128)}), f32[32768,1024]{1,0:T(8,128)}) %all-gather.3.cloned.1.call-update) | async-done | bytes 134217744 | tf_op jit(solution)/shard_map/all_gather | solution.py:58
  297.1 40.6 %reduce_sum.99 = f32[256,1024]{1,0:T(8,128)S(1)} reduce(f32[128,256,1024]{2,1,0:T(8,128)} %bitcast.6, f32[]{:T(128)} %constant.73.clone.1), dimensions={0}, to_apply=%region_0.0 | reduce | flops 33292288 | bytes 135266304 | tf_op jit(solution)/shard_map/reduce_sum | solution.py:58
  338.5 4.0 convolution_convert_fusion
  347.1 19.5 %gather_fusion.1 = f32[2048]{0:T(1024)S(1)} fusion(f32[8,16,4,512]{3,0,2,1:T(8,128)S(1)} %convolution_bitcast_fusion.1, s32[2048]{0:T(1024)S(1)} %reshape.131), kind=kCustom, calls=%fused_computation.1 | custom fusion | bytes 49152 | tf_op jit(solution)/shard_map/jit(take_along_axis)/gather | solution.py:115
  367.2 1.8 fusion.57
  369.9 1.6 fusion.145
  372.3 358.2 %while.24 = (s32[]{:T(128)}, f32[8,16,4,512]{3,2,1,0:T(4,128)}, s32[8]{0:T(128)}, s32[8]{0:T(128)}, bf16[8,4,16,64]{3,1,2,0:T(4,128)(2,1)}, /*index=5*/bf16[8,51...) while((s32[]{:T(128)}, f32[8,16,4,512]{3,2,1,0:T(4,128)}, ...), condition=%wide.region_6.7_spmd.clone, body=%wide.region_5.6_spmd.clone.sunk | while | flops 945949696 | bytes 40177104 | solution.py:108
  372.3 9.6 fusion.188
  382.8 24.6 %fusion.189 = f32[512,16,4]{1,2,0:T(4,128)} fusion(f32[16,512,512]{2,1,0:T(8,128)} %fusion.188, s32[4,512]{0,1:T(8,128)S(1)} %bitcast.130), kind=kOutput, calls=%fused_computation.16.clone.1 | convolution fusion | flops 202375168 | bytes 16916480 | tf_op jit(solution)/shard_map/while/body/eval_jaxpr/tpb,hpb->htp/dot_general | solution.py:98
  408.9 1.6 iota_compare_fusion.8
  410.6 1.7 fusion.190
  414.9 2.2 fusion.192
  417.0 9.6 fusion.188
  427.5 24.6 %fusion.189 = f32[512,16,4]{1,2,0:T(4,128)} fusion(f32[16,512,512]{2,1,0:T(8,128)} %fusion.188, s32[4,512]{0,1:T(8,128)S(1)} %bitcast.130), kind=kOutput, calls=%fused_computation.16.clone.1 | convolution fusion | flops 202375168 | bytes 16916480 | tf_op jit(solution)/shard_map/while/body/eval_jaxpr/tpb,hpb->htp/dot_general | solution.py:98
  453.7 1.6 iota_compare_fusion.8
  455.4 1.7 fusion.190
  459.7 2.2 fusion.192
  461.8 9.6 fusion.188
  472.3 24.6 %fusion.189 = f32[512,16,4]{1,2,0:T(4,128)} fusion(f32[16,512,512]{2,1,0:T(8,128)} %fusion.188, s32[4,512]{0,1:T(8,128)S(1)} %bitcast.130), kind=kOutput, calls=%fused_computation.16.clone.1 | convolution fusion | flops 202375168 | bytes 16916480 | tf_op jit(solution)/shard_map/while/body/eval_jaxpr/tpb,hpb->htp/dot_general | solution.py:98
  500.2 1.7 fusion.190
  504.4 2.1 fusion.192
  506.6 9.6 fusion.188
  517.1 24.6 %fusion.189 = f32[512,16,4]{1,2,0:T(4,128)} fusion(f32[16,512,512]{2,1,0:T(8,128)} %fusion.188, s32[4,512]{0,1:T(8,128)S(1)} %bitcast.130), kind=kOutput, calls=%fused_computation.16.clone.1 | convolution fusion | flops 202375168 | bytes 16916480 | tf_op jit(solution)/shard_map/while/body/eval_jaxpr/tpb,hpb->htp/dot_general | solution.py:98
  545.0 1.7 fusion.190
  549.2 2.2 fusion.192
  551.4 9.6 fusion.188
  561.9 24.6 %fusion.189 = f32[512,16,4]{1,2,0:T(4,128)} fusion(f32[16,512,512]{2,1,0:T(8,128)} %fusion.188, s32[4,512]{0,1:T(8,128)S(1)} %bitcast.130), kind=kOutput, calls=%fused_computation.16.clone.1 | convolution fusion | flops 202375168 | bytes 16916480 | tf_op jit(solution)/shard_map/while/body/eval_jaxpr/tpb,hpb->htp/dot_general | solution.py:98
  588.0 1.6 iota_compare_fusion.8
  589.7 1.7 fusion.190
  594.0 2.1 fusion.192
  596.1 9.6 fusion.188
  606.6 24.6 %fusion.189 = f32[512,16,4]{1,2,0:T(4,128)} fusion(f32[16,512,512]{2,1,0:T(8,128)} %fusion.188, s32[4,512]{0,1:T(8,128)S(1)} %bitcast.130), kind=kOutput, calls=%fused_computation.16.clone.1 | convolution fusion | flops 202375168 | bytes 16916480 | tf_op jit(solution)/shard_map/while/body/eval_jaxpr/tpb,hpb->htp/dot_general | solution.py:98
  634.5 1.7 fusion.190
  638.8 2.2 fusion.192
  640.9 9.6 fusion.188
  651.4 24.6 %fusion.189 = f32[512,16,4]{1,2,0:T(4,128)} fusion(f32[16,512,512]{2,1,0:T(8,128)} %fusion.188, s32[4,512]{0,1:T(8,128)S(1)} %bitcast.130), kind=kOutput, calls=%fused_computation.16.clone.1 | convolution fusion | flops 202375168 | bytes 16916480 | tf_op jit(solution)/shard_map/while/body/eval_jaxpr/tpb,hpb->htp/dot_general | solution.py:98
  679.3 1.7 fusion.190
  683.5 2.2 fusion.192
  685.7 9.6 fusion.188
  696.2 24.6 %fusion.189 = f32[512,16,4]{1,2,0:T(4,128)} fusion(f32[16,512,512]{2,1,0:T(8,128)} %fusion.188, s32[4,512]{0,1:T(8,128)S(1)} %bitcast.130), kind=kOutput, calls=%fused_computation.16.clone.1 | convolution fusion | flops 202375168 | bytes 16916480 | tf_op jit(solution)/shard_map/while/body/eval_jaxpr/tpb,hpb->htp/dot_general | solution.py:98
  724.1 1.7 fusion.190
  728.3 2.2 fusion.192
  731.9 74.3 %pmax.7 = f32[8,16,4]{2,1,0:T(8,128)S(1)} all-reduce(f32[8,16,4]{2,1,0:T(8,128)S(1)} %reduce_max.18), channel_id=1, replica_groups=mesh['req'=8,'seq'=16] {'seq'}, use_global_device_ids=true, to_apply=%region_8.9 | all-reduce | flops 512 | bytes 4096 | tf_op jit(solution)/shard_map/pmax | solution.py:130
  808.4 28.4 %while.23 = (s32[]{:T(128)}, f32[8,4,16,64]{3,1,2,0:T(4,128)}, f32[8,16,4]{1,2,0:T(4,128)S(1)}, bf16[8,512,16,64]{1,3,2,0:T(8,128)(2,1)}, f32[8,16,4,512]{3,2,1,0:T(4,128)}, /*index=5*/f32[8,16,4]{1,2,0:T(4,128)S(1)}, s32[]{:T(128)}) while((s32[]{:T(128)}, f32[8,4,16,64]{3,1,2,0:T(4,128)}, f32[8,16,4]{1,2,0:T(4,128)S(1)}, ...), condition=%wide.region_12.13_spmd, body=%wide.region_10.12_spmd.sunk | while | flops 4325314 | bytes 1351513 | solution.py:146
  809.7 2.3 fusion.180
  813.2 2.3 fusion.180
  816.8 2.3 fusion.180
  820.3 2.3 fusion.180
  823.9 2.3 fusion.180
  827.4 2.3 fusion.180
  831.0 2.3 fusion.180
  834.5 2.3 fusion.180
  836.9 69.6 %psum.22 = f32[8,16,4]{2,1,0:T(8,128)S(1)} all-reduce(f32[8,16,4]{2,1,0:T(8,128)S(1)} %copy.129), channel_id=1, replica_groups=mesh['req'=8,'seq'=16] {'seq'}, use_global_device_ids=true, to_apply=%region_14.15 | all-reduce | flops 512 | bytes 4096 | tf_op jit(solution)/shard_map/psum | solution.py:147
  907.0 77.9 %all-reduce.3.cloned.1.call-done = f32[8,4,16,64]{3,1,2,0:T(4,128)} async-done(((f32[8,4,16,64]{3,1,2,0:T(4,128)}), f32[8,4,16,64]{3,1,2,0:T(4,128)}) %all-reduce.3.cloned.1.call-update) | async-done | bytes 131088 | tf_op jit(solution)/shard_map/psum | solution.py:147
  988.2 2.3 convolution_convert_fusion.1
  990.5 80.3 %all-reduce.5.cloned.1.call-done = bf16[32,1024]{1,0:T(8,128)(2,1)} async-done(((bf16[32,1024]{1,0:T(8,128)(2,1)}), bf16[32,1024]{1,0:T(8,128)(2,1)}) %all-reduce.5.cloned.1.call-update) | async-done | bytes 65552 | tf_op jit(solution)/shard_map/psum | solution.py:166
  (249 shorter events, 84.4 us)
Async XLA Ops:
  6.5 979.9 %copy-start = (bf16[1024,1024]{1,0:T(8,128)(2,1)S(1)}, bf16[1024,1024]{1,0:T(8,128)(2,1)}, u32[]{:S(2)}) copy-start(bf16[1024,1024]{1,0:T(8,128)(2,1)} %param.25) | copy-start | bytes 6291460
  6.5 290.5 %all-gather.3.cloned.1.call-start = ((), (), s32[]{:S(2)}) async-start(), calls=%async_computation.2 | async-start | bytes 135266304 | tf_op jit(solution)/shard_map/all_gather | solution.py:58
  7.6 3.5 copy-start.1
  11.0 0.8 copy-start.16
  11.0 1.4 copy-start.17
  11.0 973.9 %all-reduce.3.cloned.1.call-start = ((), (), s32[]{:S(2)}) async-start(), calls=%async_computation | async-start | bytes 524288 | tf_op jit(solution)/shard_map/psum | solution.py:147
  12.4 325.6 %copy-start.8 = (f32[1,1024]{1,0:T(1,128)}, f32[1,1024]{1,0:T(1,128)S(1)}, u32[]{:S(2)}) copy-start(f32[1,1024]{1,0:T(1,128)S(1)} %get-tuple-element.215) | copy-start | bytes 12292
  13.0 325.0 %copy-start.10 = (f32[1,1024]{1,0:T(1,128)}, f32[1,1024]{1,0:T(1,128)S(1)}, u32[]{:S(2)}) copy-start(f32[1,1024]{1,0:T(1,128)S(1)} %get-tuple-element.219) | copy-start | bytes 12292
  16.9 2.3 copy-start.4
  19.2 0.6 copy-start.12
  19.2 0.6 copy-start.5
  337.6 4.9 copy-start.2
  337.8 0.7 copy-start.18
  338.0 0.5 copy-start.20
  372.3 436.1 %copy-start.15 = (f32[8,16,4]{1,2,0:T(4,128)S(1)}, f32[8,16,4]{1,2,0:T(4,128)}, u32[]{:S(2)}) copy-start(f32[8,16,4]{1,2,0:T(4,128)} %custom-call.5) | copy-start | bytes 6148
  408.9 3.5 copy-start.24
  408.9 4.1 copy-start.23
  453.6 3.5 copy-start.24
  453.7 4.1 copy-start.23
  498.4 3.5 copy-start.24
  498.4 4.1 copy-start.23
  543.2 3.5 copy-start.24
  543.2 4.1 copy-start.23
  588.0 3.5 copy-start.24
  588.0 4.1 copy-start.23
  632.7 3.5 copy-start.24
  632.7 4.1 copy-start.23
  677.5 3.5 copy-start.24
  677.5 4.1 copy-start.23
  722.3 3.5 copy-start.24
  722.3 4.1 copy-start.23
  808.3 98.5 %copy-start.3 = (bf16[32,1024]{1,0:T(8,128)(2,1)S(1)}, bf16[32,1024]{1,0:T(8,128)(2,1)}, u32[]{:S(2)}) copy-start(bf16[32,1024]{1,0:T(8,128)(2,1)} %get-tuple-element.208) | copy-start | bytes 196612
  836.8 149.6 %copy-start.9 = (f32[1,1024]{1,0:T(1,128)S(1)}, f32[1,1024]{1,0:T(1,128)}, u32[]{:S(2)}) copy-start(f32[1,1024]{1,0:T(1,128)} %copy-done.8) | copy-start | bytes 12292
  836.8 149.6 %copy-start.11 = (f32[1,1024]{1,0:T(1,128)S(1)}, f32[1,1024]{1,0:T(1,128)}, u32[]{:S(2)}) copy-start(f32[1,1024]{1,0:T(1,128)} %copy-done.10) | copy-start | bytes 12292
  836.8 149.6 %copy-start.19 = (f32[32]{0:T(128)S(1)}, f32[32]{0:T(128)}, u32[]{:S(2)}) copy-start(f32[32]{0:T(128)} %copy-done.18) | copy-start | bytes 388
  836.8 149.6 %copy-start.21 = (f32[32]{0:T(128)S(1)}, f32[32]{0:T(128)}, u32[]{:S(2)}) copy-start(f32[32]{0:T(128)} %copy-done.20) | copy-start | bytes 388
  906.8 164.0 %all-reduce.5.cloned.1.call-start = ((), (), s32[]{:S(2)}) async-start(), calls=%async_computation.1 | async-start | bytes 131072 | tf_op jit(solution)/shard_map/psum | solution.py:166
  986.2 2.0 copy-start.6
  986.2 2.0 copy-start.7
  986.2 2.0 copy-start.22
  986.4 86.5 %copy-start.13 = (f32[1,1024]{1,0:T(1,128)S(1)}, f32[1,1024]{1,0:T(1,128)}, u32[]{:S(2)}) copy-start(f32[1,1024]{1,0:T(1,128)} %get-tuple-element.213) | copy-start | bytes 12292
  986.4 86.5 %copy-start.14 = (f32[1,1024]{1,0:T(1,128)S(1)}, f32[1,1024]{1,0:T(1,128)}, u32[]{:S(2)}) copy-start(f32[1,1024]{1,0:T(1,128)} %get-tuple-element.217) | copy-start | bytes 12292
Sparse Core Ops, SparseCore 0:
  11.1 285.8 all-gather.2
  906.9 77.9 all-reduce.2
  990.6 80.1 all-reduce.4
